TPU v7x, 32 devices: a whole 2x2x4 slice. The times are simulated.
32 devices in a mesh: dp: 2 (over x), mp: 16 (over z, y, core).
Axes of the slice: x: 2, y: 2, z: 4, core: 2. Of those that a mesh axis runs over, the one named last changes fastest.
Arguments:
- tokens: bfloat16 [32, 512, 768], P(('dp', 'mp')), may hold values from -6 to 6
- segment_ids: int32 [32, 512], P(('dp', 'mp')), may hold values from 0 to 3, never falling along the last dimension, each value on 1 to 256 neighbouring positions
- swap_step: int32 [1], replicated, may hold values from 0 to 1023
- feature_bank: bfloat16 [8, 12, 64, 64], replicated, may hold values from -5 to 5
- query_weight: bfloat16 [768, 768], replicated, may hold values from -0.21875 to 0.21875
- query_bias: bfloat16 [768], replicated, may hold values from -1.5 to 1.5
- key_weight: bfloat16 [768, 768], replicated, may hold values from -0.21875 to 0.21875
- value_weight: bfloat16 [768, 768], replicated, may hold values from -0.21875 to 0.21875
- value_bias: bfloat16 [768], replicated, may hold values from -1.5 to 1.5
- out_weight: bfloat16 [768, 768], replicated, may hold values from -0.875 to 0.875
- out_bias: bfloat16 [768], replicated, may hold values from -1.5 to 1.5
- position_logits: bfloat16 [12, 1023], replicated, may hold values from -3 to 3
- first_gain: bfloat16 [768], replicated, may hold values from 0.5 to 1.5
- first_shift: bfloat16 [768], replicated, may hold values from -1.5 to 1.5
- up_weight: bfloat16 [768, 3072], P(None, 'mp'), may hold values from -0.21875 to 0.21875
- up_bias: bfloat16 [3072], P('mp'), may hold values from -1.5 to 1.5
- down_weight: bfloat16 [3072, 768], P('mp'), may hold values from -0.109375 to 0.109375
- down_bias: bfloat16 [768], replicated, may hold values from -1.5 to 1.5
- second_gain: bfloat16 [768], replicated, may hold values from 0.5 to 1.5
- second_shift: bfloat16 [768], replicated, may hold values from -1.5 to 1.5
- out_cotangent: bfloat16 [32, 512, 768], P(('dp', 'mp')), may hold values from -6 to 6
Outputs:
- layer_out: bfloat16 [32, 512, 768], P(('dp', 'mp'))
- grad_tokens: float32 [32, 512, 768], P(('dp', 'mp'))
- grad_query_weight: float32 [768, 768], replicated
- grad_query_bias: float32 [768], replicated
- grad_key_weight: float32 [768, 768], replicated
- grad_value_weight: float32 [768, 768], replicated
- grad_value_bias: float32 [768], replicated
- grad_out_weight: float32 [768, 768], replicated
- grad_out_bias: float32 [768], replicated
- grad_position_logits: float32 [12, 1023], replicated
- grad_first_gain: float32 [768], replicated
- grad_first_shift: float32 [768], replicated
- grad_up_weight: float32 [768, 3072], P(None, 'mp')
- grad_up_bias: float32 [3072], P('mp')
- grad_down_weight: float32 [3072, 768], P('mp')
- grad_down_bias: float32 [768], replicated
- grad_second_gain: float32 [768], replicated
- grad_second_shift: float32 [768], replicated
Inputs may be any that keep to these rules, and one draw needn't show every extreme that they name: `segment_ids`: within each row the ids never fall; a document holds at most 256 tokens.
All inputs are finite; a program needn't handle non-finite values.
Results may differ from a plain program's by a relative error of at most 0.02.
Values may be sent and summed in bfloat16 or wider, within the bound.
No kernel may reach another device: no remote copies, remote signals or barrier semaphores. Data moves between devices by JAX's collectives and lax.ppermute only.
A program may use at most 320 MiB of HBM per device.

v0:
```python
import jax
import jax.numpy as jnp
from jax import lax
from jax.sharding import PartitionSpec as P

EPSILON = 1e-05


def dot_first(left_side, right_side):
    return lax.dot_general(
        left_side, right_side, (((0,), (0,)), ((), ())), preferred_element_type=jnp.float32
    )


def dot_last(left_side, right_side):
    return lax.dot_general(
        left_side, right_side, (((1,), (1,)), ((), ())), preferred_element_type=jnp.float32
    )


def toeplitz(entries):
    head_count, span = entries.shape
    length = (span + 1) // 2
    rolled = jnp.roll(entries[:, ::-1], length, axis=1)
    tiled = jnp.tile(rolled, (1, length))[:, : length * (span - 1)]
    return tiled.reshape(head_count, length, span - 1)[:, :, :length]


def normalize(inputs, factor, offset):
    centre = inputs - jnp.mean(inputs, axis=-1, keepdims=True)
    spread = jnp.mean(centre * centre, axis=-1, keepdims=True)
    inverse = lax.rsqrt(spread + EPSILON)
    normed = centre * inverse
    return (normed * factor + offset, normed, inverse)


def norm_back(upstream, normed, inverse, factor):
    scaled = upstream * factor
    inner = (
        scaled
        - jnp.mean(scaled, axis=-1, keepdims=True)
        - normed * jnp.mean(scaled * normed, axis=-1, keepdims=True)
    )
    return (inverse * inner, jnp.sum(upstream * normed, axis=0), jnp.sum(upstream, axis=0))


def lift(row_block, projection):
    lifted = jnp.einsum("lhd,hdm->hlm", row_block, projection, preferred_element_type=jnp.float32)
    widened = row_block.astype(jnp.float32)
    squares = jnp.einsum("lhd,lhd->hl", widened, widened)
    return jnp.exp(lifted - 0.5 * squares[:, :, None]) * projection.shape[-1] ** (-0.5)


def lift_back(row_block, projection, feature, grad_feature):
    product = grad_feature.astype(jnp.float32) * feature
    rounded = product.astype(jnp.bfloat16)
    through = jnp.einsum("hlm,hdm->lhd", rounded, projection, preferred_element_type=jnp.float32)
    return through - row_block.astype(jnp.float32) * jnp.sum(product, axis=-1).T[:, :, None]


def row_scores(row_queries, row_keys, row_values, row_segments, projection, position_table):
    query_feat = lift(row_queries, projection)
    key_feat = lift(row_keys, projection)
    query_low = query_feat.astype(jnp.bfloat16)
    key_low = key_feat.astype(jnp.bfloat16)
    same_doc = (row_segments[:, None] == row_segments[None, :]).astype(jnp.float32)
    kernel = jnp.einsum("hlm,hkm->hlk", query_low, key_low, preferred_element_type=jnp.float32)
    weights = kernel * position_table * same_doc[None]
    denominator = jnp.sum(weights, axis=-1)
    weights_low = weights.astype(jnp.bfloat16)
    numerator = jnp.einsum(
        "hlk,khd->lhd", weights_low, row_values, preferred_element_type=jnp.float32
    )
    return (
        query_feat,
        key_feat,
        query_low,
        key_low,
        same_doc,
        kernel,
        weights_low,
        denominator,
        numerator,
    )


def local(
    tokens,
    segment_ids,
    swap_step,
    feature_bank,
    query_weight,
    query_bias,
    key_weight,
    value_weight,
    value_bias,
    out_weight,
    out_bias,
    position_logits,
    first_gain,
    first_shift,
    up_weight,
    up_bias,
    down_weight,
    down_bias,
    second_gain,
    second_shift,
    out_cotangent,
):
    rows_here, length, model_width = tokens.shape
    head_count = position_logits.shape[0]
    head_size = model_width // head_count
    query_scale = head_size ** (-0.25)
    token_rows = tokens.reshape(-1, model_width)
    projection = lax.dynamic_index_in_dim(
        feature_bank, swap_step[0] % feature_bank.shape[0], 0, keepdims=False
    )
    entries = jnp.exp(position_logits.astype(jnp.float32))
    position_table = toeplitz(entries)

    def by_heads(array):
        return array.reshape(rows_here, length, head_count, head_size)

    queries = (
        (
            jnp.dot(token_rows, query_weight, preferred_element_type=jnp.float32)
            + query_bias.astype(jnp.float32)
        )
        * query_scale
    ).astype(jnp.bfloat16)
    keys_all = (
        jnp.dot(token_rows, key_weight, preferred_element_type=jnp.float32) * query_scale
    ).astype(jnp.bfloat16)
    values = (
        jnp.dot(token_rows, value_weight, preferred_element_type=jnp.float32)
        + value_bias.astype(jnp.float32)
    ).astype(jnp.bfloat16)

    def forward_row(pieces):
        row_queries, row_keys, row_values, row_segments = pieces
        scores = row_scores(
            row_queries, row_keys, row_values, row_segments, projection, position_table
        )
        return (scores[8] / scores[7].T[:, :, None]).astype(jnp.bfloat16)

    mixed_out = lax.map(
        forward_row, (by_heads(queries), by_heads(keys_all), by_heads(values), segment_ids)
    ).reshape(-1, model_width)
    branch = jnp.dot(mixed_out, out_weight, preferred_element_type=jnp.float32) + out_bias.astype(
        jnp.float32
    )
    first_factor = first_gain.astype(jnp.float32)
    hidden, first_normed, first_inverse = normalize(
        token_rows.astype(jnp.float32) + branch, first_factor, first_shift.astype(jnp.float32)
    )
    hidden_low = hidden.astype(jnp.bfloat16)
    gathered = lax.all_gather(hidden_low, "mp", axis=0, tiled=True)
    upward = jnp.dot(gathered, up_weight, preferred_element_type=jnp.float32) + up_bias.astype(
        jnp.float32
    )
    activated = jax.nn.gelu(upward, approximate=False).astype(jnp.bfloat16)
    feed_out = lax.psum_scatter(
        jnp.dot(activated, down_weight, preferred_element_type=jnp.float32),
        "mp",
        scatter_dimension=0,
        tiled=True,
    )
    second_factor = second_gain.astype(jnp.float32)
    summed = hidden + feed_out + down_bias.astype(jnp.float32)
    layer_out, second_normed, second_inverse = normalize(
        summed, second_factor, second_shift.astype(jnp.float32)
    )
    upstream = out_cotangent.reshape(-1, model_width).astype(jnp.float32)
    grad_summed, grad_second_gain, grad_second_shift = norm_back(
        upstream, second_normed, second_inverse, second_factor
    )
    grad_down_bias = jnp.sum(grad_summed, axis=0)
    grad_feed = grad_summed.astype(jnp.bfloat16)

    def gelu_exact(inputs):
        return jax.nn.gelu(inputs, approximate=False)

    grad_gathered = lax.all_gather(grad_feed, "mp", axis=0, tiled=True)
    grad_act = dot_last(grad_gathered, down_weight)
    grad_upward = jax.vjp(gelu_exact, upward)[1](grad_act)[0].astype(jnp.bfloat16)
    part_up_weight = dot_first(gathered, grad_upward)
    part_down_weight = dot_first(activated, grad_gathered)
    part_up_bias = jnp.sum(grad_upward.astype(jnp.float32), axis=0)
    grad_hidden_ffn = lax.psum_scatter(
        dot_last(grad_upward, up_weight), "mp", scatter_dimension=0, tiled=True
    )
    grad_up_weight, grad_up_bias, grad_down_weight = lax.psum(
        (part_up_weight, part_up_bias, part_down_weight), "dp"
    )
    grad_hidden = grad_summed + grad_hidden_ffn
    grad_residual, grad_first_gain, grad_first_shift = norm_back(
        grad_hidden, first_normed, first_inverse, first_factor
    )
    grad_branch = grad_residual.astype(jnp.bfloat16)
    grad_out_bias = jnp.sum(grad_branch.astype(jnp.float32), axis=0)
    grad_out_weight = dot_first(mixed_out, grad_branch)
    grad_mixed = dot_last(grad_branch, out_weight).astype(jnp.bfloat16)

    def backward_row(running, pieces):
        row_queries, row_keys, row_values, row_segments, row_grad = pieces
        (
            query_feat,
            key_feat,
            query_low,
            key_low,
            same_doc,
            kernel,
            weights_low,
            denominator,
            numerator,
        ) = row_scores(row_queries, row_keys, row_values, row_segments, projection, position_table)
        spread_denom = denominator.T[:, :, None]
        grad_wide = row_grad.astype(jnp.float32)
        grad_numer = (grad_wide / spread_denom).astype(jnp.bfloat16)
        grad_denom = -jnp.einsum("lhd,lhd->hl", grad_wide, numerator / spread_denom) / denominator
        grad_weights = (
            jnp.einsum("lhd,khd->hlk", grad_numer, row_values, preferred_element_type=jnp.float32)
            + grad_denom[:, :, None]
        )
        grad_values = jnp.einsum(
            "hlk,lhd->khd", weights_low, grad_numer, preferred_element_type=jnp.float32
        ).astype(jnp.bfloat16)
        masked = grad_weights * same_doc[None]
        grad_kernel = (masked * position_table).astype(jnp.bfloat16)
        running = running + masked * kernel
        grad_qfeat = jnp.einsum(
            "hlk,hkm->hlm", grad_kernel, key_low, preferred_element_type=jnp.float32
        ).astype(jnp.bfloat16)
        grad_kfeat = jnp.einsum(
            "hlk,hlm->hkm", grad_kernel, query_low, preferred_element_type=jnp.float32
        ).astype(jnp.bfloat16)
        grad_queries = lift_back(row_queries, projection, query_feat, grad_qfeat).astype(
            jnp.bfloat16
        )
        grad_keys = lift_back(row_keys, projection, key_feat, grad_kfeat).astype(jnp.bfloat16)
        return (running, (grad_queries, grad_keys, grad_values))

    start_table = jnp.zeros((head_count, length, length), jnp.float32)
    table_grad, row_grads = lax.scan(
        backward_row,
        start_table,
        (
            by_heads(queries),
            by_heads(keys_all),
            by_heads(values),
            segment_ids,
            by_heads(grad_mixed),
        ),
    )
    grad_queries = row_grads[0].reshape(-1, model_width)
    grad_keys = row_grads[1].reshape(-1, model_width)
    grad_values = row_grads[2].reshape(-1, model_width)
    grad_query_weight = dot_first(token_rows, grad_queries) * query_scale
    grad_query_bias = jnp.sum(grad_queries.astype(jnp.float32), axis=0) * query_scale
    grad_key_weight = dot_first(token_rows, grad_keys) * query_scale
    grad_value_weight = dot_first(token_rows, grad_values)
    grad_value_bias = jnp.sum(grad_values.astype(jnp.float32), axis=0)
    grad_tokens = (
        grad_residual
        + query_scale * (dot_last(grad_queries, query_weight) + dot_last(grad_keys, key_weight))
        + dot_last(grad_values, value_weight)
    )
    toeplitz_back = jax.vjp(toeplitz, entries)[1]
    grad_logits = toeplitz_back(table_grad)[0] * entries
    shared = lax.psum(
        (
            grad_query_weight,
            grad_query_bias,
            grad_key_weight,
            grad_value_weight,
            grad_value_bias,
            grad_out_weight,
            grad_out_bias,
            grad_logits,
            grad_first_gain,
            grad_first_shift,
            grad_down_bias,
            grad_second_gain,
            grad_second_shift,
        ),
        ("dp", "mp"),
    )
    return (
        layer_out.astype(jnp.bfloat16).reshape(rows_here, length, model_width),
        grad_tokens.reshape(rows_here, length, model_width),
        shared[0],
        shared[1],
        shared[2],
        shared[3],
        shared[4],
        shared[5],
        shared[6],
        shared[7],
        shared[8],
        shared[9],
        grad_up_weight,
        grad_up_bias,
        grad_down_weight,
        shared[10],
        shared[11],
        shared[12],
    )


def solution(mesh):
    in_specs = (
        P(("dp", "mp"), None, None),
        P(("dp", "mp"), None),
        P(),
        P(),
        P(),
        P(),
        P(),
        P(),
        P(),
        P(),
        P(),
        P(),
        P(),
        P(),
        P(None, "mp"),
        P("mp"),
        P("mp", None),
        P(),
        P(),
        P(),
        P(("dp", "mp"), None, None),
    )
    out_specs = (
        P(("dp", "mp"), None, None),
        P(("dp", "mp"), None, None),
        P(),
        P(),
        P(),
        P(),
        P(),
        P(),
        P(),
        P(),
        P(),
        P(),
        P(None, "mp"),
        P("mp"),
        P("mp", None),
        P(),
        P(),
        P(),
    )
    return jax.shard_map(local, mesh=mesh, in_specs=in_specs, out_specs=out_specs, check_vma=False)
```

profile of v0, /device:TPU:8, one launch (start us, length us, event | category | flops | bytes accessed | tf_op | source)
XLA Modules:
  0.0 1372.5 jit_solution(12590324390042866375)
XLA Ops:
  9.5 3.2 multiply_convert_fusion.3
  14.4 3.0 multiply_convert_fusion.2
  20.0 11.5 tile.4
  31.5 38.0 %tile.10 = f32[12,523776]{1,0:T(8,128)} reshape(f32[12,512,1023]{2,1,0:T(8,128)} %tile.4) | data formatting | bytes 50282496 | tf_op jit(solution)/shard_map/tile | solution.py:25
  69.5 22.6 %slice.28 = f32[12,523264]{1,0:T(8,128)} slice(f32[12,523776]{1,0:T(8,128)} %tile.10), slice={[0:12], [0:523264]} | slice | bytes 50233344 | tf_op jit(solution)/shard_map/slice | solution.py:25
  92.1 42.2 %reshape.182 = f32[12,512,1022]{2,1,0:T(8,128)} reshape(f32[12,523264]{1,0:T(8,128)} %slice.28) | data formatting | bytes 50233344 | tf_op jit(solution)/shard_map/reshape | solution.py:26
  134.3 10.7 slice.29
  145.0 12.6 copy.112
  158.7 3.2 add_convert_fusion.2
  161.8 2.4 copy.57
  166.5 9.4 fusion.7
  175.9 2.3 fusion.59
  182.2 100.6 %all-gather.3.cloned.1.call-done = bf16[8192,768]{1,0:T(8,128)(2,1)} async-done(((bf16[512,768]{1,0:T(8,128)(2,1)}), bf16[8192,768]{1,0:T(8,128)(2,1)}) %all-gather.3.cloned.1.call-update) | async-done | bytes 12582928 | tf_op jit(solution)/shard_map/all_gather | solution.py:157
  282.8 20.5 %multiply_convert_fusion.1 = (bf16[8192,192]{0,1:T(8,128)(2,1)S(1)}, f32[8192,192]{0,1:T(8,128)}, f32[8192,192]{0,1:T(8,128)}) fusion(f32[192]{0:T(256)S(1)} %convert_element_type.196, bf16[8192,768]{1,0:T(8,128)(2,1)} %all-gather.3.cloned.1.call-done, bf16[768,192]{0,1:T(8,128)(2,1)} %param.35), kind=kOutput, calls=%fused_computation.9 | convolution fusion | flops 2519728128 | bytes 28607232 | tf_op jit(solution)/shard_map/dot_general | solution.py:158
  305.1 10.1 fusion.63
  315.9 240.6 %reduce-scatter.3.cloned.1.call-done = f32[512,768]{1,0:T(8,128)} async-done(((f32[8192,768]{1,0:T(8,128)}), f32[512,768]{1,0:T(8,128)}) %reduce-scatter.3.cloned.1.call-update) | async-done | bytes 1572880 | tf_op jit(solution)/shard_map/reduce_scatter | solution.py:162
  560.9 2.1 fusion.55
  565.2 100.3 %all-gather.5.cloned.1.call-done = bf16[8192,768]{1,0:T(8,128)(2,1)} async-done(((bf16[512,768]{1,0:T(8,128)(2,1)}), bf16[8192,768]{1,0:T(8,128)(2,1)}) %all-gather.5.cloned.1.call-update) | async-done | bytes 12582928 | tf_op jit(solution)/shard_map/all_gather | solution.py:183
  665.5 10.9 convert_reduce_fusion
  678.1 10.1 fusion.64
  688.7 240.8 %reduce-scatter.5.cloned.1.call-done = f32[512,768]{1,0:T(8,128)} async-done(((f32[8192,768]{1,0:T(8,128)}), f32[512,768]{1,0:T(8,128)}) %reduce-scatter.5.cloned.1.call-update) | async-done | bytes 1572880 | tf_op jit(solution)/shard_map/reduce_scatter | solution.py:189
  929.5 3.3 multiply_reduce_fusion
  935.6 2.2 fusion.51
  940.1 5.7 convert_reduce_fusion.3
  945.8 18.3 %fusion = (f32[12,512,512]{1,2,0:T(8,128)}, bf16[12,512,512]{1,2,0:T(8,128)(2,1)}) fusion(f32[12,512,512]{1,2,0:T(8,128)} %get-tuple-element.152, f32[12,512]{1,0:T(8,128)S(1)} %negate_divide_fusion, f32[512,512]{0,1:T(8,128)} %compare_convert_fusion, f32[12,512,512]{1,2,0:T(8,128)} %copy.112, bf16[512,12,64]{0,2,1:T(8,128)(2,1)} %bitcast.162, ...), kind=kOutput, calls=%fused_computation.3 | convolution fusion | flops 419561472 | bytes 46710784 | tf_op jit(solution)/shard_map/while/body/eval_jaxpr/lhd,khd->hlk/dot_general | solution.py:222
  964.1 4.1 fusion.61
  968.7 2.0 fusion.62
  970.8 2.2 convolution_bitcast_fusion
  973.3 2.2 multiply_bitcast_fusion
  976.8 2.2 multiply_bitcast_fusion.1
  980.9 5.6 psum.123
  986.5 9.4 fusion.67
  995.9 8.2 fusion.68
  1004.2 12.8 copy.113
  1017.0 14.6 %pad.14.clone = f32[12,512,1022]{2,1,0:T(8,128)} pad(f32[12,512,512]{2,1,0:T(8,128)} %copy.113, f32[]{:T(128)} %constant.51.clone.1), padding=0_0x0_0x0_510 | pad | bytes 37699588 | tf_op jit(solution)/shard_map/transpose(jvp())/pad | solution.py:26
  1031.6 47.0 %reshape.189 = f32[12,523264]{1,0:T(8,128)} reshape(f32[12,512,1022]{2,1,0:T(8,128)} %pad.14.clone) | data formatting | bytes 50233344 | tf_op jit(solution)/shard_map/transpose(jvp())/reshape | solution.py:26
  1078.6 22.9 %pad.15 = f32[12,523776]{1,0:T(8,128)} pad(f32[12,523264]{1,0:T(8,128)} %reshape.189, f32[]{:T(128)} %constant.51.clone.1), padding=0_0x0_512 | pad | bytes 50257924 | tf_op jit(solution)/shard_map/transpose(jvp())/pad | solution.py:25
  1101.5 43.8 %reshape.190 = f32[12,512,1023]{2,1,0:T(8,128)} reshape(f32[12,523776]{1,0:T(8,128)} %pad.15) | data formatting | bytes 50282496 | tf_op jit(solution)/shard_map/transpose(jvp())/reshape | solution.py:25
  1145.4 9.2 reduce_sum.214
  1157.3 3.4 fusion.66
  1162.7 4.5 add_bitcast_fusion
  1167.3 3.8 all-reduce.13.cloned.1.call-done
  1171.1 3.0 copy.71
  1174.1 3.0 copy.72
  1177.2 3.0 copy.73
  1180.2 36.7 %all-reduce.15.cloned.1.call-done = (f32[768,192]{0,1:T(8,128)}, f32[192,768]{1,0:T(8,128)}) async-done(((f32[768,192]{0,1:T(8,128)}, f32[192,768]{1,0:T(8,128)}), (f32[768,192]{0,1:T(8,128)}, f32[192,768]{1,0:T(8,128)})) %all-reduce.15.cloned.1.call-update) | async-done | bytes 1179664 | tf_op jit(solution)/shard_map/psum | solution.py:192
  1216.9 136.8 %all-reduce.11.cloned.1.call-done = (f32[768]{0:T(1024)}, f32[768]{0:T(1024)}, f32[768]{0:T(1024)}, f32[12,1023]{1,0:T(8,128)}, f32[768]{0:T(1024)}, /*index=5*/...) async-done(((f32[768]{0:T(1024)}, f32[768]{0:T(1024)}, f32[768]{0:T(1024)}, f32[12,1023]{1,0:T(8,128)}, f32[768]{0:T(1024)}, /*index=5*/f32[768]{0:T(1024)}, ...) | async-done | bytes 73696 | tf_op jit(solution)/shard_map/psum | solution.py:270
  1356.3 3.3 copy.132
  (193 shorter events, 46.4 us)
Async XLA Ops:
  7.2 157.0 %copy-start = (bf16[8,12,64,64]{3,2,1,0:T(8,128)(2,1)S(1)}, bf16[8,12,64,64]{3,2,1,0:T(8,128)(2,1)}, u32[]{:S(2)}) copy-start(bf16[8,12,64,64]{3,2,1,0:T(8,128)(2,1)} %param.24) | copy-start | bytes 2359300
  7.2 275.6 %all-gather.3.cloned.1.call-start = ((), (), s32[]{:S(2)}) async-start(), calls=%async_computation.2 | async-start | bytes 13369344 | tf_op jit(solution)/shard_map/all_gather | solution.py:157
  8.8 3.9 copy-start.34
  12.7 1.7 copy-start.17
  14.2 150.0 %copy-start.9 = (bf16[512,768]{0,1:T(8,128)(2,1)}, bf16[512,768]{0,1:T(8,128)(2,1)S(1)}, u32[]{:S(2)}) copy-start(bf16[512,768]{0,1:T(8,128)(2,1)S(1)} %copy.58) | copy-start | bytes 2359300
  17.4 2.2 slice-start.1
  18.8 145.9 %copy-start.11 = (bf16[512,768]{0,1:T(8,128)(2,1)}, bf16[512,768]{0,1:T(8,128)(2,1)S(1)}, u32[]{:S(2)}) copy-start(bf16[512,768]{0,1:T(8,128)(2,1)S(1)} %copy.60) | copy-start | bytes 2359300
  145.0 12.6 copy-start.37
  145.0 13.7 copy-start.44
  161.8 2.4 copy-start.45
  164.7 11.2 copy-start.2
  164.7 1.8 copy-start.13
  166.5 9.4 copy-start.4
  166.5 9.4 copy-start.26
  175.9 3.3 copy-start.20
  175.9 3.3 copy-start.18
  175.9 3.3 copy-start.51
  182.1 374.4 %reduce-scatter.3.cloned.1.call-start = ((), (), s32[]{:S(2)}) async-start(), calls=%async_computation.3 | async-start | bytes 26738688 | tf_op jit(solution)/shard_map/reduce_scatter | solution.py:162
  182.1 123.0 %copy-start.32 = (bf16[192,768]{1,0:T(8,128)(2,1)S(1)}, bf16[192,768]{1,0:T(8,128)(2,1)}, u32[]{:S(2)}) copy-start(bf16[192,768]{1,0:T(8,128)(2,1)} %param.37) | copy-start | bytes 884740
  303.3 1.8 copy-start.21
  315.2 350.3 %all-gather.5.cloned.1.call-start = ((), (), s32[]{:S(2)}) async-start(), calls=%async_computation.4 | async-start | bytes 13369344 | tf_op jit(solution)/shard_map/all_gather | solution.py:183
  565.2 364.3 %reduce-scatter.5.cloned.1.call-start = ((), (), s32[]{:S(2)}) async-start(), calls=%async_computation.5 | async-start | bytes 26738688 | tf_op jit(solution)/shard_map/reduce_scatter | solution.py:189
  665.5 12.5 copy-start.33
  688.2 482.9 %all-reduce.13.cloned.1.call-start = ((), (), s32[]{:S(2)}) async-start(), calls=%async_computation.7 | async-start | bytes 18874368 | tf_op jit(solution)/shard_map/psum | solution.py:270
  938.1 7.7 copy-start.16
  945.8 18.3 %copy-start.3 = (f32[12,512,64]{1,2,0:T(8,128)S(1)}, f32[12,512,64]{1,2,0:T(8,128)}, u32[]{:S(2)}) copy-start(f32[12,512,64]{1,2,0:T(8,128)} %copy-done.2) | copy-start | bytes 4718596
  945.8 18.3 %copy-start.5 = (f32[12,512,64]{1,2,0:T(8,128)S(1)}, f32[12,512,64]{1,2,0:T(8,128)}, u32[]{:S(2)}) copy-start(f32[12,512,64]{1,2,0:T(8,128)} %copy-done.4) | copy-start | bytes 4718596
  964.1 4.6 copy-start.1
  968.7 2.0 copy-start.19
  968.7 2.0 copy-start.27
  970.8 2.2 copy-start.12
  973.3 2.2 copy-start.10
  979.1 237.9 %all-reduce.15.cloned.1.call-start = ((), (), s32[]{:S(2)}) async-start(), calls=%async_computation.8 | async-start | bytes 2359296 | tf_op jit(solution)/shard_map/psum | solution.py:192
  986.5 9.4 copy-start.23
  1004.1 349.6 %all-reduce.11.cloned.1.call-start = ((), (), s32[]{:S(2)}) async-start(), calls=%async_computation.6 | async-start | bytes 196608 | tf_op jit(solution)/shard_map/psum | solution.py:270
  1145.4 11.2 copy-start.35
  1157.3 3.4 copy-start.25
  1157.3 3.4 copy-start.53
  1160.7 2.0 copy-start.8
  1356.3 3.3 copy-start.43
  1356.3 3.9 copy-start.36
  1356.3 4.6 copy-start.42
  1356.3 5.2 copy-start.41
  1356.3 5.7 copy-start.31
  1359.6 3.3 copy-start.30
  1359.6 4.1 copy-start.40
  1359.6 4.7 copy-start.39
  1359.6 5.3 copy-start.38
  (16 other events, 17.2 us)
Sparse Core Ops, SparseCore 0:
  182.2 100.5 all-gather.2
  315.3 241.1 reduce-scatter.2
  565.3 100.1 all-gather.4
  688.3 241.0 reduce-scatter.4
  979.2 191.8 all-reduce.12
  1173.9 42.9 all-reduce.14
  1225.0 128.6 all-reduce.10
where the time goes:
time: 1380 us; the launch traced here: 1370 us
  waiting for transfers between devices  860 us (62%)
  local copies, waits for them, and re-layouts  320 us (23%)
  matrix products  142 us (10%)
  other arithmetic  28.3 us (2%)
  between operations  15.7 us (1%)
    reduce_scatter x1, waiting for transfers between devices, local(): lax.psum_scatter(dot_last(grad_upward, up_weight), 'mp', scatter_dimensio...  241 us
    reduce_scatter x1, waiting for transfers between devices, local(): lax.psum_scatter(jnp.dot(activated, down_weight, preferred_element_type=j...  241 us
    psum x2, waiting for transfers between devices, local(): lax.psum((grad_query_weight, grad_query_bias, grad_key_weight, grad_value...  141 us
    all_gather x1, waiting for transfers between devices, local(): gathered = lax.all_gather(hidden_low, 'mp', axis=0, tiled=True)  101 us
    all_gather x1, waiting for transfers between devices, local(): grad_gathered = lax.all_gather(grad_feed, 'mp', axis=0, tiled=True)  100 us
    reshape x2, local copies, waits for them, and re-layouts, toeplitz(): return tiled.reshape(head_count, length, span - 1)[:, :, :length]  89.2 us
    unnamed x130, local copies, waits for them, and re-layouts  59.4 us
    another operation x2, local copies, waits for them, and re-layouts, toeplitz(): tiled = jnp.tile(rolled, (1, length))[:, :length * (span - 1)]  49.6 us
  transfers between devices with their start and end apart: 7, of which 7 were waited for; matrix products, arithmetic and copies ran while one was open for 14% of the time, Pallas kernels for 0%

commit v1 on v0

--- a/solution.py
+++ b/solution.py
@@ -154,7 +154,26 @@
         token_rows.astype(jnp.float32) + branch, first_factor, first_shift.astype(jnp.float32)
     )
     hidden_low = hidden.astype(jnp.bfloat16)
-    gathered = lax.all_gather(hidden_low, "mp", axis=0, tiled=True)
+    now, e_next, outcome_arr = (lax.axis_size("mp"), lax.axis_index("mp"), hidden_low.shape[0])
+    newest = mixed_arr = hidden_low
+    gathered = lax.dynamic_update_slice_in_dim(
+        jnp.zeros(
+            [h * now if dd == 0 else h for dd, h in enumerate(hidden_low.shape)], hidden_low.dtype
+        ),
+        hidden_low,
+        e_next * outcome_arr,
+        axis=0,
+    )
+    for tick in range(1, now // 2 + 1):
+        newest = lax.ppermute(newest, "mp", [(dd, (dd + 1) % now) for dd in range(now)])
+        gathered = lax.dynamic_update_slice_in_dim(
+            gathered, newest, (e_next - tick) % now * outcome_arr, axis=0
+        )
+        if 2 * tick < now:
+            mixed_arr = lax.ppermute(mixed_arr, "mp", [(dd, (dd - 1) % now) for dd in range(now)])
+            gathered = lax.dynamic_update_slice_in_dim(
+                gathered, mixed_arr, (e_next + tick) % now * outcome_arr, axis=0
+            )
     upward = jnp.dot(gathered, up_weight, preferred_element_type=jnp.float32) + up_bias.astype(
         jnp.float32
     )

time: 1380 us -> 1430 us (1.036)
  starting transfers between devices: 0.69 us -> 103 us
  waiting for transfers between devices: 860 us -> 784 us
  local copies, waits for them, and re-layouts: 320 us -> 345 us
    ppermute x0 -> x15, starting transfers between devices: none -> 102 us  [the longest x8 99.2 us: local(): lax.ppermute(newest, 'mp', [(dd, (dd + 1) % now) for dd in range(now)])]
    all_gather x1 -> x0, waiting for transfers between devices: 101 us -> none  [local(): gathered = lax.all_gather(hidden_low, 'mp', axis=0, tiled=True)]
    ppermute x0 -> x15, waiting for transfers between devices: none -> 21.5 us  [the longest x8 21.5 us: local(): lax.ppermute(newest, 'mp', [(dd, (dd + 1) % now) for dd in range(now)])]
    dynamic_update_slice x0 -> x15, local copies, waits for them, and re-layouts: none -> 21.2 us  [the longest x8 11.1 us: local(): lax.dynamic_update_slice_in_dim(gathered, newest, (e_next - tick) % now *...]
    unnamed x130 -> x154, local copies, waits for them, and re-layouts: 59.4 us -> 58.3 us
  transfers between devices with their start and end apart: 7 -> 21, of which waited for: 7 -> 11; matrix products, arithmetic and copies ran while one was open for 14% -> 15% of each run, Pallas kernels for 0% -> 0%
where the time goes in v1:
time: 1430 us
  waiting for transfers between devices  784 us (55%)
  local copies, waits for them, and re-layouts  345 us (24%)
  matrix products  140 us (10%)
  starting transfers between devices  103 us (7%)
  other arithmetic  34.8 us (2%)
  between operations  15.8 us (1%)
    reduce_scatter x1, waiting for transfers between devices, local(): lax.psum_scatter(jnp.dot(activated, down_weight, preferred_element_type=j...  246 us
    reduce_scatter x1, waiting for transfers between devices, local(): lax.psum_scatter(dot_last(grad_upward, up_weight), 'mp', scatter_dimensio...  241 us
    psum x2, waiting for transfers between devices, local(): lax.psum((grad_query_weight, grad_query_bias, grad_key_weight, grad_value...  139 us
    all_gather x1, waiting for transfers between devices, local(): grad_gathered = lax.all_gather(grad_feed, 'mp', axis=0, tiled=True)  100 us
    ppermute x8, starting transfers between devices, local(): lax.ppermute(newest, 'mp', [(dd, (dd + 1) % now) for dd in range(now)])  99.2 us
    reshape x2, local copies, waits for them, and re-layouts, toeplitz(): return tiled.reshape(head_count, length, span - 1)[:, :, :length]  89.3 us
    unnamed x154, local copies, waits for them, and re-layouts  58.3 us
    another operation x2, local copies, waits for them, and re-layouts, toeplitz(): tiled = jnp.tile(rolled, (1, length))[:, :length * (span - 1)]  49.6 us
  transfers between devices with their start and end apart: 21, of which 11 were waited for; matrix products, arithmetic and copies ran while one was open for 15% of the time, Pallas kernels for 0%

profile of v1, /device:TPU:8, one launch (start us, length us, event | category | flops | bytes accessed | tf_op | source)
XLA Modules:
  0.0 1428.2 jit_solution(3226191657664535763)
XLA Ops:
  9.5 3.2 multiply_convert_fusion.3
  20.0 11.5 tile.4
  31.5 38.1 %tile.10 = f32[12,523776]{1,0:T(8,128)} reshape(f32[12,512,1023]{2,1,0:T(8,128)} %tile.4) | data formatting | bytes 50282496 | tf_op jit(solution)/shard_map/tile | solution.py:25
  69.6 22.6 %slice.28 = f32[12,523264]{1,0:T(8,128)} slice(f32[12,523776]{1,0:T(8,128)} %tile.10), slice={[0:12], [0:523264]} | slice | bytes 50233344 | tf_op jit(solution)/shard_map/slice | solution.py:25
  92.1 42.3 %reshape.182 = f32[12,512,1022]{2,1,0:T(8,128)} reshape(f32[12,523264]{1,0:T(8,128)} %slice.28) | data formatting | bytes 50233344 | tf_op jit(solution)/shard_map/reshape | solution.py:26
  134.4 10.6 slice.29
  145.0 12.6 copy.112
  158.7 3.2 add_convert_fusion.2
  165.5 9.3 fusion.7
  179.4 5.3 broadcast_in_dim.30
  188.6 9.8 collective-permute-done
  198.3 6.6 collective-permute-start.2
  205.0 5.8 collective-permute-done.2
  211.6 13.3 collective-permute-start.4
  226.8 17.1 %collective-permute-start.6 = (bf16[512,768]{1,0:T(8,128)(2,1)S(1)}, bf16[512,768]{1,0:T(8,128)(2,1)S(1)}, u32[]{:S(2)}, u32[]{:S(2)}) collective-permute-start(bf16[512,768]{1,0:T(8,128)(2,1)S(1)} %collective-permute-done.4), channel_id=1, source_target_pairs={{0,1},{1,2},{2,3},{3,4},{4,5},{5,6},{6,7},{7,8},{8,9},{9,10},{10,1... | collective-permute-start | bytes 2359304 | tf_op jit(solution)/shard_map/ppermute | solution.py:168
  245.9 15.9 %collective-permute-start.8 = (bf16[512,768]{1,0:T(8,128)(2,1)S(1)}, bf16[512,768]{1,0:T(8,128)(2,1)}, u32[]{:S(2)}, u32[]{:S(2)}) collective-permute-start(bf16[512,768]{1,0:T(8,128)(2,1)S(1)} %collective-permute-done.6), channel_id=1, source_target_pairs={{0,1},{1,2},{2,3},{3,4},{4,5},{5,6},{6,7},{7,8},{8,9},{9,10},{10,1... | collective-permute-start | bytes 2359304 | tf_op jit(solution)/shard_map/ppermute | solution.py:168
  264.0 17.1 %collective-permute-start.10 = (bf16[512,768]{1,0:T(8,128)(2,1)}, bf16[512,768]{1,0:T(8,128)(2,1)}, u32[]{:S(2)}, u32[]{:S(2)}) collective-permute-start(bf16[512,768]{1,0:T(8,128)(2,1)} %collective-permute-done.8), channel_id=1, source_target_pairs={{0,1},{1,2},{2,3},{3,4},{4,5},{5,6},{6,7},{7,8},{8,9},{9,10},{10,1... | collective-permute-start | bytes 2359304 | tf_op jit(solution)/shard_map/ppermute | solution.py:168
  285.4 15.9 %collective-permute-start.12 = (bf16[512,768]{1,0:T(8,128)(2,1)}, bf16[512,768]{1,0:T(8,128)(2,1)S(1)}, u32[]{:S(2)}, u32[]{:S(2)}) collective-permute-start(bf16[512,768]{1,0:T(8,128)(2,1)} %collective-permute-done.10), channel_id=1, source_target_pairs={{0,1},{1,2},{2,3},{3,4},{4,5},{5,6},{6,7},{7,8},{8,9},{9,10},{10,1... | collective-permute-start | bytes 2359304 | tf_op jit(solution)/shard_map/ppermute | solution.py:168
  308.2 13.3 collective-permute-start.14
  331.5 20.5 %multiply_convert_fusion.1 = (bf16[8192,192]{0,1:T(8,128)(2,1)S(1)}, f32[8192,192]{0,1:T(8,128)}, f32[8192,192]{0,1:T(8,128)}) fusion(f32[192]{0:T(256)S(1)} %convert_element_type.196, bf16[8192,768]{1,0:T(8,128)(2,1)} %constant_dynamic-update-slice_fusion, bf16[768,192]{0,1:T(8,128)(2,1)S(1)} %copy-done.44), kind=kOutput, calls=%fused_computation.9 | convolution fusion | flops 2519728128 | bytes 28607232 | tf_op jit(solution)/shard_map/dot_general | solution.py:177
  353.8 10.2 fusion.64
  364.7 245.5 %reduce-scatter.3.cloned.1.call-done = f32[512,768]{1,0:T(8,128)} async-done(((f32[8192,768]{1,0:T(8,128)}), f32[512,768]{1,0:T(8,128)}) %reduce-scatter.3.cloned.1.call-update) | async-done | bytes 1572880 | tf_op jit(solution)/shard_map/reduce_scatter | solution.py:181
  618.2 100.3 %all-gather.2.cloned.1.call-done = bf16[8192,768]{1,0:T(8,128)(2,1)} async-done(((bf16[512,768]{1,0:T(8,128)(2,1)}), bf16[8192,768]{1,0:T(8,128)(2,1)}) %all-gather.2.cloned.1.call-update) | async-done | bytes 12582928 | tf_op jit(solution)/shard_map/all_gather | solution.py:202
  718.5 7.2 fusion.65
  725.7 6.3 convert_reduce_fusion
  733.7 10.2 fusion.66
  744.3 240.8 %reduce-scatter.5.cloned.1.call-done = f32[512,768]{1,0:T(8,128)} async-done(((f32[8192,768]{1,0:T(8,128)}), f32[512,768]{1,0:T(8,128)}) %reduce-scatter.5.cloned.1.call-update) | async-done | bytes 1572880 | tf_op jit(solution)/shard_map/reduce_scatter | solution.py:208
  985.2 3.3 multiply_reduce_fusion
  995.8 5.7 convert_reduce_fusion.3
  1001.5 18.3 %fusion = (f32[12,512,512]{1,2,0:T(8,128)}, bf16[12,512,512]{1,2,0:T(8,128)(2,1)}) fusion(f32[12,512,512]{1,2,0:T(8,128)} %get-tuple-element.154, f32[12,512]{1,0:T(8,128)S(1)} %negate_divide_fusion, f32[512,512]{0,1:T(8,128)} %compare_convert_fusion, f32[12,512,512]{1,2,0:T(8,128)} %copy.112, bf16[512,12,64]{0,2,1:T(8,128)(2,1)} %bitcast.162, ...), kind=kOutput, calls=%fused_computation.3 | convolution fusion | flops 419561472 | bytes 46710784 | tf_op jit(solution)/shard_map/while/body/eval_jaxpr/lhd,khd->hlk/dot_general | solution.py:241
  1019.9 4.1 fusion.62
  1036.7 5.6 psum.123
  1042.4 9.4 fusion.70
  1051.8 8.2 fusion.69
  1060.0 12.7 copy.113
  1072.7 14.7 %pad.14.clone = f32[12,512,1022]{2,1,0:T(8,128)} pad(f32[12,512,512]{2,1,0:T(8,128)} %copy.113, f32[]{:T(128)} %constant.191.clone.1), padding=0_0x0_0x0_510 | pad | bytes 37699588 | tf_op jit(solution)/shard_map/transpose(jvp())/pad | solution.py:26
  1087.4 47.0 %reshape.189 = f32[12,523264]{1,0:T(8,128)} reshape(f32[12,512,1022]{2,1,0:T(8,128)} %pad.14.clone) | data formatting | bytes 50233344 | tf_op jit(solution)/shard_map/transpose(jvp())/reshape | solution.py:26
  1134.4 22.9 %pad.15 = f32[12,523776]{1,0:T(8,128)} pad(f32[12,523264]{1,0:T(8,128)} %reshape.189, f32[]{:T(128)} %constant.191.clone.1), padding=0_0x0_512 | pad | bytes 50257924 | tf_op jit(solution)/shard_map/transpose(jvp())/pad | solution.py:25
  1157.4 43.9 %reshape.190 = f32[12,512,1023]{2,1,0:T(8,128)} reshape(f32[12,523776]{1,0:T(8,128)} %pad.15) | data formatting | bytes 50282496 | tf_op jit(solution)/shard_map/transpose(jvp())/reshape | solution.py:25
  1201.3 9.2 reduce_sum.214
  1213.2 3.3 fusion.68
  1216.5 3.2 fusion.67
  1219.7 4.5 add_bitcast_fusion
  1226.9 3.0 copy.71
  1230.0 3.0 copy.72
  1236.1 36.7 %all-reduce.15.cloned.1.call-done = (f32[768,192]{0,1:T(8,128)}, f32[192,768]{1,0:T(8,128)}) async-done(((f32[768,192]{0,1:T(8,128)}, f32[192,768]{1,0:T(8,128)}), (f32[768,192]{0,1:T(8,128)}, f32[192,768]{1,0:T(8,128)})) %all-reduce.15.cloned.1.call-update) | async-done | bytes 1179664 | tf_op jit(solution)/shard_map/psum | solution.py:211
  1272.8 136.6 %all-reduce.11.cloned.1.call-done = (f32[768]{0:T(1024)}, f32[768]{0:T(1024)}, f32[768]{0:T(1024)}, f32[12,1023]{1,0:T(8,128)}, f32[768]{0:T(1024)}, /*index=5*/...) async-done(((f32[768]{0:T(1024)}, f32[768]{0:T(1024)}, f32[768]{0:T(1024)}, f32[12,1023]{1,0:T(8,128)}, f32[768]{0:T(1024)}, /*index=5*/f32[768]{0:T(1024)}, ...) | async-done | bytes 73696 | tf_op jit(solution)/shard_map/psum | solution.py:289
  1412.0 3.3 copy.148
  (261 shorter events, 99.3 us)
Async XLA Ops:
  7.2 157.0 %copy-start = (bf16[8,12,64,64]{3,2,1,0:T(8,128)(2,1)S(1)}, bf16[8,12,64,64]{3,2,1,0:T(8,128)(2,1)}, u32[]{:S(2)}) copy-start(bf16[8,12,64,64]{3,2,1,0:T(8,128)(2,1)} %param.24) | copy-start | bytes 2359300
  7.2 603.0 %reduce-scatter.3.cloned.1.call-start = ((), (), s32[]{:S(2)}) async-start(), calls=%async_computation.2 | async-start | bytes 26738688 | tf_op jit(solution)/shard_map/reduce_scatter | solution.py:181
  14.2 150.0 %copy-start.10 = (bf16[512,768]{0,1:T(8,128)(2,1)}, bf16[512,768]{0,1:T(8,128)(2,1)S(1)}, u32[]{:S(2)}) copy-start(bf16[512,768]{0,1:T(8,128)(2,1)S(1)} %copy.58) | copy-start | bytes 2359300
  18.9 145.9 %copy-start.12 = (bf16[512,768]{0,1:T(8,128)(2,1)}, bf16[512,768]{0,1:T(8,128)(2,1)S(1)}, u32[]{:S(2)}) copy-start(bf16[512,768]{0,1:T(8,128)(2,1)S(1)} %copy.60) | copy-start | bytes 2359300
  145.0 12.6 copy-start.49
  145.0 13.8 copy-start.56
  164.7 10.1 copy-start.2
  165.5 9.3 copy-start.4
  165.5 9.3 copy-start.25
  184.7 96.4 %copy-start.66 = (bf16[192]{0:T(256)(128)(2,1)S(1)}, bf16[192]{0:T(256)(128)(2,1)}, u32[]{:S(2)}) copy-start(bf16[192]{0:T(256)(128)(2,1)} %param.36) | copy-start | bytes 1156
  185.9 12.4 collective-permute-start
  185.9 19.0 %collective-permute-start.1 = (bf16[512,768]{1,0:T(8,128)(2,1)S(1)}, bf16[512,768]{1,0:T(8,128)(2,1)S(1)}, u32[]{:S(2)}, u32[]{:S(2)}) collective-permute-start(bf16[512,768]{1,0:T(8,128)(2,1)S(1)} %get-tuple-element.148), channel_id=1, source_target_pairs={{0,15},{1,0},{2,1},{3,2},{4,3},{5,4},{6,5},{7,6},{8,7},{9,8},{10,9... | collective-permute-start | bytes 2359304 | tf_op jit(solution)/shard_map/ppermute | solution.py:173
  198.3 6.6 copy-start.37
  198.3 12.4 collective-permute-start.2
  205.0 21.8 %copy-start.32 = (bf16[512,768]{1,0:T(8,128)(2,1)}, bf16[512,768]{1,0:T(8,128)(2,1)S(1)}, u32[]{:S(2)}) copy-start(bf16[512,768]{1,0:T(8,128)(2,1)S(1)} %collective-permute-done.1) | copy-start | bytes 2359300
  205.0 19.9 %collective-permute-start.3 = (bf16[512,768]{1,0:T(8,128)(2,1)S(1)}, bf16[512,768]{1,0:T(8,128)(2,1)S(1)}, u32[]{:S(2)}, u32[]{:S(2)}) collective-permute-start(bf16[512,768]{1,0:T(8,128)(2,1)S(1)} %collective-permute-done.1), channel_id=1, source_target_pairs={{0,15},{1,0},{2,1},{3,2},{4,3},{5,4},{6,5},{7,6},{8,7},{9,8},{10,9... | collective-permute-start | bytes 2359304 | tf_op jit(solution)/shard_map/ppermute | solution.py:173
  211.6 15.2 %collective-permute-start.4 = (bf16[512,768]{1,0:T(8,128)(2,1)S(1)}, bf16[512,768]{1,0:T(8,128)(2,1)S(1)}, u32[]{:S(2)}, u32[]{:S(2)}) collective-permute-start(bf16[512,768]{1,0:T(8,128)(2,1)S(1)} %collective-permute-done.2), channel_id=1, source_target_pairs={{0,1},{1,2},{2,3},{3,4},{4,5},{5,6},{6,7},{7,8},{8,9},{9,10},{10,1... | collective-permute-start | bytes 2359304 | tf_op jit(solution)/shard_map/ppermute | solution.py:168
  224.9 19.1 %copy-start.33 = (bf16[512,768]{1,0:T(8,128)(2,1)}, bf16[512,768]{1,0:T(8,128)(2,1)S(1)}, u32[]{:S(2)}) copy-start(bf16[512,768]{1,0:T(8,128)(2,1)S(1)} %collective-permute-done.3) | copy-start | bytes 2359300
  224.9 19.1 %collective-permute-start.5 = (bf16[512,768]{1,0:T(8,128)(2,1)S(1)}, bf16[512,768]{1,0:T(8,128)(2,1)S(1)}, u32[]{:S(2)}, u32[]{:S(2)}) collective-permute-start(bf16[512,768]{1,0:T(8,128)(2,1)S(1)} %collective-permute-done.3), channel_id=1, source_target_pairs={{0,15},{1,0},{2,1},{3,2},{4,3},{5,4},{6,5},{7,6},{8,7},{9,8},{10,9... | collective-permute-start | bytes 2359304 | tf_op jit(solution)/shard_map/ppermute | solution.py:173
  226.8 17.1 %copy-start.35 = (bf16[512,768]{1,0:T(8,128)(2,1)}, bf16[512,768]{1,0:T(8,128)(2,1)S(1)}, u32[]{:S(2)}) copy-start(bf16[512,768]{1,0:T(8,128)(2,1)S(1)} %collective-permute-done.4) | copy-start | bytes 2359300
  226.8 19.1 %collective-permute-start.6 = (bf16[512,768]{1,0:T(8,128)(2,1)S(1)}, bf16[512,768]{1,0:T(8,128)(2,1)S(1)}, u32[]{:S(2)}, u32[]{:S(2)}) collective-permute-start(bf16[512,768]{1,0:T(8,128)(2,1)S(1)} %collective-permute-done.4), channel_id=1, source_target_pairs={{0,1},{1,2},{2,3},{3,4},{4,5},{5,6},{6,7},{7,8},{8,9},{9,10},{10,1... | collective-permute-start | bytes 2359304 | tf_op jit(solution)/shard_map/ppermute | solution.py:168
  244.0 17.8 %collective-permute-start.7 = (bf16[512,768]{1,0:T(8,128)(2,1)S(1)}, bf16[512,768]{1,0:T(8,128)(2,1)}, u32[]{:S(2)}, u32[]{:S(2)}) collective-permute-start(bf16[512,768]{1,0:T(8,128)(2,1)S(1)} %collective-permute-done.5), channel_id=1, source_target_pairs={{0,15},{1,0},{2,1},{3,2},{4,3},{5,4},{6,5},{7,6},{8,7},{9,8},{10,9... | collective-permute-start | bytes 2359304 | tf_op jit(solution)/shard_map/ppermute | solution.py:173
  245.9 15.9 %copy-start.40 = (bf16[512,768]{1,0:T(8,128)(2,1)}, bf16[512,768]{1,0:T(8,128)(2,1)S(1)}, u32[]{:S(2)}) copy-start(bf16[512,768]{1,0:T(8,128)(2,1)S(1)} %collective-permute-done.6) | copy-start | bytes 2359300
  245.9 18.1 %collective-permute-start.8 = (bf16[512,768]{1,0:T(8,128)(2,1)S(1)}, bf16[512,768]{1,0:T(8,128)(2,1)}, u32[]{:S(2)}, u32[]{:S(2)}) collective-permute-start(bf16[512,768]{1,0:T(8,128)(2,1)S(1)} %collective-permute-done.6), channel_id=1, source_target_pairs={{0,1},{1,2},{2,3},{3,4},{4,5},{5,6},{6,7},{7,8},{8,9},{9,10},{10,1... | collective-permute-start | bytes 2359304 | tf_op jit(solution)/shard_map/ppermute | solution.py:168
  261.8 21.5 %collective-permute-start.9 = (bf16[512,768]{1,0:T(8,128)(2,1)}, bf16[512,768]{1,0:T(8,128)(2,1)}, u32[]{:S(2)}, u32[]{:S(2)}) collective-permute-start(bf16[512,768]{1,0:T(8,128)(2,1)} %collective-permute-done.7), channel_id=1, source_target_pairs={{0,15},{1,0},{2,1},{3,2},{4,3},{5,4},{6,5},{7,6},{8,7},{9,8},{10,9... | collective-permute-start | bytes 2359304 | tf_op jit(solution)/shard_map/ppermute | solution.py:173
  264.0 21.5 %collective-permute-start.10 = (bf16[512,768]{1,0:T(8,128)(2,1)}, bf16[512,768]{1,0:T(8,128)(2,1)}, u32[]{:S(2)}, u32[]{:S(2)}) collective-permute-start(bf16[512,768]{1,0:T(8,128)(2,1)} %collective-permute-done.8), channel_id=1, source_target_pairs={{0,1},{1,2},{2,3},{3,4},{4,5},{5,6},{6,7},{7,8},{8,9},{9,10},{10,1... | collective-permute-start | bytes 2359304 | tf_op jit(solution)/shard_map/ppermute | solution.py:168
  281.1 20.3 %copy-start.31 = (bf16[512,768]{1,0:T(8,128)(2,1)S(1)}, bf16[512,768]{1,0:T(8,128)(2,1)}, u32[]{:S(2)}) copy-start(bf16[512,768]{1,0:T(8,128)(2,1)} %copy-done.30) | copy-start | bytes 2359300
  281.1 21.2 %copy-start.34 = (bf16[512,768]{1,0:T(8,128)(2,1)S(1)}, bf16[512,768]{1,0:T(8,128)(2,1)}, u32[]{:S(2)}) copy-start(bf16[512,768]{1,0:T(8,128)(2,1)} %copy-done.33) | copy-start | bytes 2359300
  283.3 20.0 %copy-start.36 = (bf16[512,768]{1,0:T(8,128)(2,1)S(1)}, bf16[512,768]{1,0:T(8,128)(2,1)}, u32[]{:S(2)}) copy-start(bf16[512,768]{1,0:T(8,128)(2,1)} %copy-done.35) | copy-start | bytes 2359300
  283.3 22.8 %collective-permute-start.11 = (bf16[512,768]{1,0:T(8,128)(2,1)}, bf16[512,768]{1,0:T(8,128)(2,1)S(1)}, u32[]{:S(2)}, u32[]{:S(2)}) collective-permute-start(bf16[512,768]{1,0:T(8,128)(2,1)} %collective-permute-done.9), channel_id=1, source_target_pairs={{0,15},{1,0},{2,1},{3,2},{4,3},{5,4},{6,5},{7,6},{8,7},{9,8},{10,9... | collective-permute-start | bytes 2359304 | tf_op jit(solution)/shard_map/ppermute | solution.py:173
  285.4 18.8 %copy-start.39 = (bf16[512,768]{1,0:T(8,128)(2,1)S(1)}, bf16[512,768]{1,0:T(8,128)(2,1)}, u32[]{:S(2)}) copy-start(bf16[512,768]{1,0:T(8,128)(2,1)} %copy-done.38) | copy-start | bytes 2359300
  285.4 22.7 %collective-permute-start.12 = (bf16[512,768]{1,0:T(8,128)(2,1)}, bf16[512,768]{1,0:T(8,128)(2,1)S(1)}, u32[]{:S(2)}, u32[]{:S(2)}) collective-permute-start(bf16[512,768]{1,0:T(8,128)(2,1)} %collective-permute-done.10), channel_id=1, source_target_pairs={{0,1},{1,2},{2,3},{3,4},{4,5},{5,6},{6,7},{7,8},{8,9},{9,10},{10,1... | collective-permute-start | bytes 2359304 | tf_op jit(solution)/shard_map/ppermute | solution.py:168
  306.1 23.5 %collective-permute-start.13 = (bf16[512,768]{1,0:T(8,128)(2,1)S(1)}, bf16[512,768]{1,0:T(8,128)(2,1)S(1)}, u32[]{:S(2)}, u32[]{:S(2)}) collective-permute-start(bf16[512,768]{1,0:T(8,128)(2,1)S(1)} %collective-permute-done.11), channel_id=1, source_target_pairs={{0,15},{1,0},{2,1},{3,2},{4,3},{5,4},{6,5},{7,6},{8,7},{9,8},{10,9... | collective-permute-start | bytes 2359304 | tf_op jit(solution)/shard_map/ppermute | solution.py:173
  308.2 22.4 %collective-permute-start.14 = (bf16[512,768]{1,0:T(8,128)(2,1)S(1)}, bf16[512,768]{1,0:T(8,128)(2,1)S(1)}, u32[]{:S(2)}, u32[]{:S(2)}) collective-permute-start(bf16[512,768]{1,0:T(8,128)(2,1)S(1)} %collective-permute-done.12), channel_id=1, source_target_pairs={{0,1},{1,2},{2,3},{3,4},{4,5},{5,6},{6,7},{7,8},{8,9},{9,10},{10,1... | collective-permute-start | bytes 2359304 | tf_op jit(solution)/shard_map/ppermute | solution.py:168
  331.5 22.3 %copy-start.27 = (bf16[192,768]{1,0:T(8,128)(2,1)S(1)}, bf16[192,768]{1,0:T(8,128)(2,1)}, u32[]{:S(2)}) copy-start(bf16[192,768]{1,0:T(8,128)(2,1)} %param.37) | copy-start | bytes 884740
  364.0 354.5 %all-gather.2.cloned.1.call-start = ((), (), s32[]{:S(2)}) async-start(), calls=%async_computation.3 | async-start | bytes 13369344 | tf_op jit(solution)/shard_map/all_gather | solution.py:202
  618.1 367.0 %reduce-scatter.5.cloned.1.call-start = ((), (), s32[]{:S(2)}) async-start(), calls=%async_computation.4 | async-start | bytes 26738688 | tf_op jit(solution)/shard_map/reduce_scatter | solution.py:208
  725.7 8.0 copy-start.45
  743.9 483.0 %all-reduce.13.cloned.1.call-start = ((), (), s32[]{:S(2)}) async-start(), calls=%async_computation.6 | async-start | bytes 18874368 | tf_op jit(solution)/shard_map/psum | solution.py:289
  993.8 7.8 copy-start.17
  1001.5 18.3 %copy-start.3 = (f32[12,512,64]{1,2,0:T(8,128)S(1)}, f32[12,512,64]{1,2,0:T(8,128)}, u32[]{:S(2)}) copy-start(f32[12,512,64]{1,2,0:T(8,128)} %copy-done.2) | copy-start | bytes 4718596
  1001.5 18.3 %copy-start.5 = (f32[12,512,64]{1,2,0:T(8,128)S(1)}, f32[12,512,64]{1,2,0:T(8,128)}, u32[]{:S(2)}) copy-start(f32[12,512,64]{1,2,0:T(8,128)} %copy-done.4) | copy-start | bytes 4718596
  1034.9 237.9 %all-reduce.15.cloned.1.call-start = ((), (), s32[]{:S(2)}) async-start(), calls=%async_computation.7 | async-start | bytes 2359296 | tf_op jit(solution)/shard_map/psum | solution.py:211
  1042.4 9.4 copy-start.23
  1059.9 349.4 %all-reduce.11.cloned.1.call-start = ((), (), s32[]{:S(2)}) async-start(), calls=%async_computation.5 | async-start | bytes 196608 | tf_op jit(solution)/shard_map/psum | solution.py:289
  1201.2 11.2 copy-start.47
  1411.9 5.8 copy-start.43
  1412.0 6.6 copy-start.42
  (42 other events, 115.5 us)
Sparse Core Ops, SparseCore 0:
  364.1 246.0 reduce-scatter.2
  618.3 100.2 all-gather.1
  744.0 241.0 reduce-scatter.4
  1035.0 191.8 all-reduce.12
  1229.7 42.9 all-reduce.14
  1280.7 128.6 all-reduce.10
